TPU v7x, 256 devices: a whole 4x4x8 slice. The times are simulated.
256 devices in a mesh: req: 32 (over y, x, z_hi), tp: 8 (over z_lo, core).
Axes of the slice: x: 4, y: 4, z: 8 (z_hi: 2, z_lo: 4; z = z_hi * 4 + z_lo), core: 2. Of those that a mesh axis runs over, the one named last changes fastest.
Arguments:
- residual: bfloat16 [8192, 2304], P('req'), may hold values from -58 to 58
- context: bfloat16 [8192, 2304], P('req', 'tp'), may hold values from -6 to 6
- attention_output_weight: bfloat16 [2304, 2304], P('tp'), may hold values from -0.1875 to 0.1875
- adapter_down_maps: bfloat16 [64, 2304, 16], P('req', 'tp'), may hold values from -0.125 to 0.125
- adapter_up_maps: bfloat16 [64, 16, 2304], P('req'), may hold values from -1.5 to 1.5
- adapter_storage_row: int32 [64], replicated, may hold values from 0 to 63, each once
- active_adapters: int32 [16], replicated, may hold values from 0 to 63, as said below
- request_token_length: int32 [32, 4], P('req'), may hold values from 1 to 128, 256 in all within a row
- request_adapter_entry: int32 [32, 4], P('req'), may hold values from 0 to 15
- expert_norm_gain: bfloat16 [2304], replicated, may hold values from 0.099609375 to 1.8984375
- router_projection: bfloat16 [2304, 8], replicated, may hold values from -0.125 to 0.125
- expert_choice_pairs: int32 [8192, 2], P('req'), may hold values from 0 to 7, all different within a row; in each aligned block of 256 rows (0 to 255, 256 to 511, ...) at most 80 rows name the same one
- expert_gate_weight: bfloat16 [32, 2304, 5760], P('req', None, 'tp'), as said below
- expert_up_weight: bfloat16 [32, 2304, 5760], P('req', None, 'tp'), as said below
- expert_down_weight: bfloat16 [32, 5760, 2304], P('req', 'tp'), as said below
Outputs:
- layer_out: bfloat16 [8192, 2304], P('req', 'tp')
Inputs may be any that keep to these rules, and one draw needn't show every extreme that they name: `active_adapters`: 16 different adapter numbers, 0 and 63 among them. `adapter_storage_row`: every stored row appears once. `request_token_length`: each group's lengths sum to 256; the longest request of a group has exactly half of 256 tokens. `expert_choice_pairs`: each row names two different experts; within the 256 rows of one group no expert is named by more than 80 rows, a bound that some block reaches. `expert_gate_weight`: the 4 holders c * 8 + e of expert e hold the same weights. `expert_up_weight`: the 4 holders c * 8 + e of expert e hold the same weights. `expert_down_weight`: the 4 holders c * 8 + e of expert e hold the same weights.
All inputs are finite; a program needn't handle non-finite values.
Results may differ from a plain program's by a relative error of at most 0.0095.
Values may be sent and summed in bfloat16 or wider, within the bound.
A program may use at most 128 MiB of HBM per device.

v0:
```python
import jax
import jax.numpy as jnp
from jax import lax
from jax.sharding import PartitionSpec as P

CAP = 80
NORM_EPS = 1e-05


def adapter_onehot(request_token_length, request_adapter_entry, active_count, token_count):
    bounds = jnp.cumsum(request_token_length[0])
    position = jnp.arange(token_count, dtype=jnp.int32)
    segment = jnp.sum((position[:, None] >= bounds[None, :]).astype(jnp.int32), axis=1)
    slot_range = jnp.arange(request_token_length.shape[1], dtype=jnp.int32)
    segment_hot = (segment[:, None] == slot_range[None, :]).astype(jnp.int32)
    token_pick = jnp.sum(segment_hot * request_adapter_entry[0][None, :], axis=1)
    return token_pick[:, None] == jnp.arange(active_count, dtype=jnp.int32)[None, :]


def route_tables(expert_choice_pairs, expert_count, capacity):
    expert_ids = jnp.arange(expert_count, dtype=jnp.int32)
    first_hit = expert_choice_pairs[None, :, 0] == expert_ids[:, None]
    second_hit = expert_choice_pairs[None, :, 1] == expert_ids[:, None]
    chosen = first_hit | second_hit
    slot_of = jnp.cumsum(chosen.astype(jnp.int32), axis=1) - 1
    slot_range = jnp.arange(capacity, dtype=jnp.int32)
    placement = chosen[:, None, :] & (slot_of[:, None, :] == slot_range[None, :, None])
    return (placement, first_hit, second_hit)


def on_device(
    residual,
    context,
    attention_output_weight,
    adapter_down_maps,
    adapter_up_maps,
    adapter_storage_row,
    active_adapters,
    request_token_length,
    request_adapter_entry,
    expert_norm_gain,
    router_projection,
    expert_choice_pairs,
    expert_gate_weight,
    expert_up_weight,
    expert_down_weight,
):
    token_count = residual.shape[0]
    hidden_width = residual.shape[1]
    active_count = active_adapters.shape[0]
    adapter_rank_size = adapter_down_maps.shape[2]
    stored_rows = adapter_storage_row[active_adapters]
    all_down, all_up = (
        lax.all_gather(adapter_down_maps, "req", axis=0, tiled=True),
        lax.all_gather(adapter_up_maps, "req", axis=0, tiled=True),
    )
    active_down = all_down[stored_rows]
    active_up = all_up[stored_rows]
    adapter_indicator = adapter_onehot(
        request_token_length, request_adapter_entry, active_count, token_count
    )
    down_joined = jnp.transpose(active_down, (1, 0, 2)).reshape(
        context.shape[1], active_count * adapter_rank_size
    )
    up_joined = active_up.reshape(active_count * adapter_rank_size, hidden_width)
    low_all = jnp.dot(context, down_joined, preferred_element_type=jnp.float32)
    reduced_mask = jnp.repeat(adapter_indicator, adapter_rank_size, axis=1)
    low_rank = jnp.where(reduced_mask, low_all, 0.0).astype(jnp.bfloat16)
    head_part = jnp.dot(
        context, attention_output_weight, preferred_element_type=jnp.float32
    ) + jnp.dot(low_rank, up_joined, preferred_element_type=jnp.float32)
    share_width = hidden_width // lax.axis_size("tp")
    share_start = lax.axis_index("tp") * share_width
    gain_all = expert_norm_gain.astype(jnp.float32)
    head_sum = lax.psum(head_part.astype(jnp.bfloat16), "tp").astype(jnp.float32)
    blended_rows = residual.astype(jnp.float32) + head_sum
    mean_square = jnp.mean(blended_rows * blended_rows, axis=1, keepdims=True)
    normed = (blended_rows * lax.rsqrt(mean_square + NORM_EPS) * gain_all).astype(jnp.bfloat16)
    mixed_share = lax.dynamic_slice_in_dim(blended_rows, share_start, share_width, 1)
    logits = jnp.dot(normed, router_projection, preferred_element_type=jnp.float32)
    expert_count = router_projection.shape[1]
    expert_range = jnp.arange(expert_count, dtype=jnp.int32)
    logit_first = jnp.sum(
        jnp.where(expert_choice_pairs[:, 0:1] == expert_range[None, :], logits, 0.0), axis=1
    )
    logit_second = jnp.sum(
        jnp.where(expert_choice_pairs[:, 1:2] == expert_range[None, :], logits, 0.0), axis=1
    )
    weight_first = 1.0 / (1.0 + jnp.exp(logit_second - logit_first))
    weight_second = 1.0 / (1.0 + jnp.exp(logit_first - logit_second))
    copy_count = lax.axis_size("req") // expert_count
    quota_slots = CAP // copy_count
    placement, first_hit, second_hit = route_tables(expert_choice_pairs, expert_count, CAP)
    holder_place = jnp.transpose(
        placement.reshape(expert_count, copy_count, quota_slots, token_count), (1, 0, 2, 3)
    ).reshape(copy_count * expert_count, quota_slots, token_count)
    send_rows = jnp.einsum(
        "hqt,td->hqd", holder_place.astype(jnp.bfloat16), normed, preferred_element_type=jnp.float32
    ).astype(jnp.bfloat16)
    gate_local = expert_gate_weight[0]
    up_local = expert_up_weight[0]
    down_local = expert_down_weight[0]
    rows_in = lax.all_to_all(send_rows, "req", split_axis=0, concat_axis=0, tiled=True)
    gate_value = jnp.einsum("nqd,df->nqf", rows_in, gate_local, preferred_element_type=jnp.float32)
    up_value = jnp.einsum("nqd,df->nqf", rows_in, up_local, preferred_element_type=jnp.float32)
    hidden = (jax.nn.silu(gate_value) * up_value).astype(jnp.bfloat16)
    partial_value = jnp.einsum(
        "nqf,fd->nqd", hidden, down_local, preferred_element_type=jnp.float32
    )
    token_weight = jnp.where(first_hit, weight_first[None, :], 0.0) + jnp.where(
        second_hit, weight_second[None, :], 0.0
    )
    holder_weight = jnp.tile(token_weight, (copy_count, 1))
    scaled_place = holder_place.astype(jnp.float32) * holder_weight[:, None, :]
    returned = lax.all_to_all(
        partial_value.astype(jnp.bfloat16), "req", split_axis=0, concat_axis=0, tiled=True
    )
    contribution = jnp.einsum(
        "hqt,hqd->td",
        scaled_place,
        returned.astype(jnp.float32),
        precision=lax.Precision.HIGHEST,
        preferred_element_type=jnp.float32,
    )
    moe_share = lax.psum_scatter(
        contribution.astype(jnp.bfloat16), "tp", scatter_dimension=1, tiled=True
    ).astype(jnp.float32)
    return (mixed_share + moe_share).astype(jnp.bfloat16)


def solution(mesh):
    return jax.shard_map(
        on_device,
        mesh=mesh,
        in_specs=(
            P("req", None),
            P("req", "tp"),
            P("tp", None),
            P("req", "tp", None),
            P("req", None, None),
            P(),
            P(),
            P("req", None),
            P("req", None),
            P(),
            P(),
            P("req", None),
            P("req", None, "tp"),
            P("req", None, "tp"),
            P("req", "tp", None),
        ),
        out_specs=P("req", "tp"),
        check_vma=False,
    )
```

profile of v0, /device:TPU:4, one launch (start us, length us, event | category | flops | bytes accessed | tf_op | source)
XLA Modules:
  0.0 505.3 jit_solution(13145580559629970987)
XLA Ops:
  6.5 0.0 copy-start
  6.5 0.0 all-gather.2.cloned.1.call-start
  6.5 0.7 all-gather.2.cloned.1.call-update
  7.3 0.0 all-reduce.2.cloned.1.call-start
  7.3 0.9 convert_element_type.53
  8.2 1.3 reduce-window.18
  9.6 0.8 fusion.41
  10.3 0.6 reduce-window.19
  10.9 0.2 slice_reduce_fusion
  11.2 0.0 copy-start.4
  11.2 0.7 compare_select_fusion.1
  11.8 1.3 gather_fusion
  13.2 136.1 %all_gather.6 = bf16[64,288,16]{1,2,0:T(8,128)(2,1)} all-gather(bf16[2,288,16]{1,2,0:T(8,128)(2,1)} %param.18), channel_id=1, replica_groups=mesh['req'=32,'tp'=8] {'req'}, dimensions={0}, use_global_device_ids=true | all-gather | bytes 608256 | tf_op jit(solution)/shard_map/all_gather | solution.py:54
  149.3 1.7 gather_fusion.1
  151.0 0.7 convert_reduce_fusion
  151.7 0.7 select_reduce_fusion.2
  152.5 3.7 fusion.42
  156.1 0.0 copy-done.4
  156.1 0.0 all-gather.2.cloned.1.call-done
  156.2 4.0 gather_fusion.2
  160.1 0.6 broadcast_in_dim.27
  160.8 0.0 slice-start
  160.8 3.9 fusion.1
  164.7 0.0 all-reduce.2.cloned.1.call-update
  164.8 0.1 copy.29
  164.9 0.0 slice-done
  164.9 0.1 add_bitcast_fusion
  165.0 77.7 %all-reduce.2.cloned.1.call-done = bf16[256,2304]{1,0:T(8,128)(2,1)} async-done(((bf16[256,2304]{1,0:T(8,128)(2,1)}), bf16[256,2304]{1,0:T(8,128)(2,1)}) %all-reduce.2.cloned.1.call-update) | async-done | bytes 1179664 | tf_op jit(solution)/shard_map/psum | solution.py:75
  242.6 0.0 copy-start.1
  242.6 0.0 copy-start.2
  242.6 3.6 convert_add_fusion
  246.2 0.0 copy-done.1
  246.2 0.0 copy-done.2
  246.2 1.2 convolution_convert_fusion.1
  247.4 1.6 copy.30
  249.0 0.0 copy-start.5
  249.0 91.9 %all_to_all.10 = bf16[32,20,2304]{2,1,0:T(8,128)(2,1)S(1)} all-to-all(bf16[32,20,2304]{2,1,0:T(8,128)(2,1)S(1)} %copy.30), channel_id=1, replica_groups=mesh['req'=32,'tp'=8] {'req'}, dimensions={0} | all-to-all | bytes 5898240 | tf_op jit(solution)/shard_map/all_to_all | solution.py:103
  340.9 0.0 copy-start.3
  340.9 1.8 copy-done.3
  342.7 0.0 copy-done.5
  342.7 3.8 fusion.6
  346.5 0.0 copy-done
  346.5 11.1 %convolution_convert_fusion = bf16[32,20,2304]{2,0,1:T(8,128)(2,1)} fusion(bf16[1,720,2304]{2,1,0:T(8,128)(2,1)S(1)} %copy-done, f32[32,20,720]{2,0,1:T(8,128)} %fusion.6, bf16[1,2304,720]{1,2,0:T(8,128)(2,1)} %param.28, bf16[32,20,2304]{2,1,0:T(8,128)(2,1)} %copy-done.3), kind=kOutput, calls=%fused_computation.3 | convolution fusion | flops 4250972160 | bytes 14376960 | tf_op jit(solution)/shard_map/nqf,fd->nqd/dot_general | solution.py:107
  357.6 5.3 %copy.33 = bf16[32,20,2304]{2,1,0:T(8,128)(2,1)} copy(bf16[32,20,2304]{2,0,1:T(8,128)(2,1)} %convolution_convert_fusion) | data formatting | bytes 5898240 | tf_op jit(solution)/shard_map/convert_element_type | solution.py:116
  362.9 0.0 copy-start.6
  362.9 8.3 %all-to-all-start.1 = ((bf16[32,20,2304]{2,1,0:T(8,128)(2,1)}), bf16[32,20,2304]{2,1,0:T(8,128)(2,1)}, u32[]{:S(2)}, u32[]{:S(2)}) async-start(bf16[32,20,2304]{2,1,0:T(8,128)(2,1)} %copy.33), calls=%async_computation.1 | async-start | bytes 7077888 | tf_op jit(solution)/shard_map/all_to_all | solution.py:115
  371.2 0.3 reduce-scatter.4.cloned.1.call-start
  371.5 0.0 copy-done.6
  371.5 2.2 select_reduce_fusion.1
  373.8 67.8 %all-to-all-done.1 = bf16[32,20,2304]{2,1,0:T(8,128)(2,1)} async-done(((bf16[32,20,2304]{2,1,0:T(8,128)(2,1)}), bf16[32,20,2304]{2,1,0:T(8,128)(2,1)}, u32[]{:S(2)}, u32[]{:S(2)}) %all-to-all-start.1) | async-done | bytes 2949152 | tf_op jit(solution)/shard_map/all_to_all | solution.py:115
  441.5 6.8 %fusion.2 = bf16[2304,256]{1,0:T(8,128)(2,1)} fusion(bf16[32,20,2304]{2,1,0:T(8,128)(2,1)} %all-to-all-done.1, f32[32,256]{1,0:T(8,128)S(1)} %broadcast_bitcast_fusion, s32[32,20]{0,1:T(8,128)S(1)} %copy.29, s32[32,256]{1,0:T(8,128)S(1)} %broadcast_bitcast_fusion.1, pred[32,256]{1,0:T(8,128)(4,1)S(1)} %broadcast_bitcast_fusion.2), kind=kOutput, calls=%fused_computation.9 | convolution fusion | flops 4530929664 | bytes 4205056 | tf_op jit(solution)/shard_map/hqt,hqd->td/dot_general | solution.py:118
  448.3 0.0 reduce-scatter.4.cloned.1.call-update
  448.3 45.8 %reduce-scatter.4.cloned.1.call-done = bf16[288,256]{1,0:T(8,128)(2,1)} async-done(((bf16[2304,256]{1,0:T(8,128)(2,1)}), bf16[288,256]{1,0:T(8,128)(2,1)}) %reduce-scatter.4.cloned.1.call-update) | async-done | bytes 147472
  494.1 1.1 copy.38
  495.2 1.9 add_convert_fusion
  497.1 1.7 copy.36
  (15 shorter events, 0.1 us)
Async XLA Ops:
  6.5 340.0 %copy-start = (bf16[1,720,2304]{2,1,0:T(8,128)(2,1)S(1)}, bf16[1,720,2304]{2,1,0:T(8,128)(2,1)}, u32[]{:S(2)}) copy-start(bf16[1,720,2304]{2,1,0:T(8,128)(2,1)} %param.29) | copy-start | bytes 9953284
  6.5 149.6 %all-gather.2.cloned.1.call-start = ((), (), s32[]{:S(2)}) async-start(), calls=%async_computation.3 | async-start | bytes 4866048 | tf_op jit(solution)/shard_map/all_gather | solution.py:55
  7.3 235.3 %all-reduce.2.cloned.1.call-start = ((), (), s32[]{:S(2)}) async-start(), calls=%async_computation.4 | async-start | bytes 2359296 | tf_op jit(solution)/shard_map/psum | solution.py:75
  11.2 145.0 %copy-start.4 = (s32[8,3]{0,1:T(4,128)}, s32[8,3]{0,1:T(4,128)S(1)}, u32[]{:S(2)}) copy-start(s32[8,3]{0,1:T(4,128)S(1)} %reduce-window.20) | copy-start | bytes 292
  160.8 4.1 slice-start
  242.6 3.6 copy-start.1
  242.6 3.6 copy-start.2
  249.0 93.7 %copy-start.5 = (bf16[1,2304,720]{1,2,0:T(8,128)(2,1)S(1)}, bf16[1,2304,720]{1,2,0:T(8,128)(2,1)}, u32[]{:S(2)}) copy-start(bf16[1,2304,720]{1,2,0:T(8,128)(2,1)} %param.27) | copy-start | bytes 9953284
  340.9 1.8 copy-start.3
  362.9 8.6 %copy-start.6 = (bf16[2304,8]{0,1:T(8,128)(2,1)S(1)}, bf16[2304,8]{0,1:T(8,128)(2,1)}, u32[]{:S(2)}) copy-start(bf16[2304,8]{0,1:T(8,128)(2,1)} %param.25) | copy-start | bytes 110596
  362.9 78.7 %all-to-all-start.1 = ((bf16[32,20,2304]{2,1,0:T(8,128)(2,1)}), bf16[32,20,2304]{2,1,0:T(8,128)(2,1)}, u32[]{:S(2)}, u32[]{:S(2)}) async-start(bf16[32,20,2304]{2,1,0:T(8,128)(2,1)} %copy.33), calls=%async_computation.1 | async-start | bytes 7077888 | tf_op jit(solution)/shard_map/all_to_all | solution.py:115
  371.2 122.9 %reduce-scatter.4.cloned.1.call-start = ((), (), s32[]{:S(2)}) async-start(), calls=%async_computation.5 | async-start | bytes 1327104
Sparse Core Ops, SparseCore 0:
  10.8 132.5 all-gather.1
  164.9 77.7 all-reduce.1
  448.4 45.6 reduce-scatter.3
where the time goes:
time: 506 us; the launch traced here: 505 us
  blocking collectives  228 us (45%)
  waiting for transfers between devices  192 us (38%)
  matrix products  32.6 us (6%)
  local copies, waits for them, and re-layouts  20.3 us (4%)
  between operations  13.2 us (3%)
  other arithmetic  10.6 us (2%)
  starting transfers between devices  8.62 us (2%)
    all_gather x1, blocking collectives, on_device(): lax.all_gather(adapter_down_maps, 'req', axis=0, tiled=True)  136 us
    all_to_all x1, blocking collectives, on_device(): lax.all_to_all(send_rows, 'req', split_axis=0, concat_axis=0, tiled=True)  91.9 us
    psum x1, waiting for transfers between devices, on_device(): lax.psum(head_part.astype(jnp.bfloat16), 'tp').astype(jnp.float32)  77.7 us
    all_to_all x1, waiting for transfers between devices, on_device(): lax.all_to_all(partial_value.astype(jnp.bfloat16), 'req', split_axis=0, c...  67.8 us
    unnamed x4, waiting for transfers between devices  46.5 us
    dot_general x1, matrix products, on_device(): jnp.einsum('nqf,fd->nqd', hidden, down_local, preferred_element_type=jnp....  11.1 us
  transfers between devices with their start and end apart: 4, of which 3 were waited for; matrix products, arithmetic and copies ran while one was open for 3% of the time, Pallas kernels for 0%

commit v1 on v0

--- a/solution.py
+++ b/solution.py
@@ -51,7 +51,10 @@
     adapter_rank_size = adapter_down_maps.shape[2]
     stored_rows = adapter_storage_row[active_adapters]
     all_down, all_up = (
-        lax.all_gather(adapter_down_maps, "req", axis=0, tiled=True),
+        jnp.concatenate(
+            lax.all_to_all(jnp.stack([adapter_down_maps] * lax.axis_size("req")), "req", 0, 0),
+            axis=0,
+        ),
         lax.all_gather(adapter_up_maps, "req", axis=0, tiled=True),
     )
     active_down = all_down[stored_rows]

time: 506 us -> 474 us (0.937)
  blocking collectives: 228 us -> 91.9 us
  waiting for transfers between devices: 192 us -> 285 us
  starting transfers between devices: 8.62 us -> 22.9 us
    all_gather x1 -> x0, blocking collectives: 136 us -> none  [on_device(): lax.all_gather(adapter_down_maps, 'req', axis=0, tiled=True)]
    all_gather x1, waiting for transfers between devices: 0.01 us -> 89.3 us  [on_device(): lax.all_gather(adapter_up_maps, 'req', axis=0, tiled=True)]
    all_to_all x0 -> x1, waiting for transfers between devices: none -> 14.5 us  [on_device(): lax.all_to_all(jnp.stack([adapter_down_maps] * lax.axis_size('req')), 're...]
    all_to_all x0 -> x1, starting transfers between devices: none -> 14.3 us  [on_device(): lax.all_to_all(jnp.stack([adapter_down_maps] * lax.axis_size('req')), 're...]
    psum x1, waiting for transfers between devices: 77.7 us -> 69.9 us  [on_device(): lax.psum(head_part.astype(jnp.bfloat16), 'tp').astype(jnp.float32)]
  transfers between devices with their start and end apart: 4 -> 5, of which waited for: 3 -> 5; matrix products, arithmetic and copies ran while one was open for 3% -> 2% of each run, Pallas kernels for 0% -> 0%
where the time goes in v1:
time: 474 us; the launch traced here: 473 us
  waiting for transfers between devices  285 us (60%)
  blocking collectives  91.9 us (19%)
  matrix products  32.5 us (7%)
  starting transfers between devices  22.9 us (5%)
  local copies, waits for them, and re-layouts  20.8 us (4%)
  between operations  13.4 us (3%)
  other arithmetic  6.58 us (1%)
    all_to_all x1, blocking collectives, on_device(): lax.all_to_all(send_rows, 'req', split_axis=0, concat_axis=0, tiled=True)  91.9 us
    all_gather x1, waiting for transfers between devices, on_device(): lax.all_gather(adapter_up_maps, 'req', axis=0, tiled=True)  89.3 us
    psum x1, waiting for transfers between devices, on_device(): lax.psum(head_part.astype(jnp.bfloat16), 'tp').astype(jnp.float32)  69.9 us
    all_to_all x1, waiting for transfers between devices, on_device(): lax.all_to_all(partial_value.astype(jnp.bfloat16), 'req', split_axis=0, c...  65.8 us
    unnamed x4, waiting for transfers between devices  45.6 us
    all_to_all x1, waiting for transfers between devices, on_device(): lax.all_to_all(jnp.stack([adapter_down_maps] * lax.axis_size('req')), 're...  14.5 us
    all_to_all x1, starting transfers between devices, on_device(): lax.all_to_all(jnp.stack([adapter_down_maps] * lax.axis_size('req')), 're...  14.3 us
    dot_general x1, matrix products, on_device(): jnp.einsum('nqf,fd->nqd', hidden, down_local, preferred_element_type=jnp....  11.1 us
  transfers between devices with their start and end apart: 5, of which 5 were waited for; matrix products, arithmetic and copies ran while one was open for 2% of the time, Pallas kernels for 0%

profile of v1, /device:TPU:4, one launch (start us, length us, event | category | flops | bytes accessed | tf_op | source)
XLA Modules:
  0.0 473.2 jit_solution(10943472928631821262)
XLA Ops:
  6.5 0.0 copy-start
  6.5 0.0 copy-start.8
  6.5 0.0 copy-start.13
  6.5 0.0 copy-start.6
  6.5 0.0 copy-start.1
  6.6 0.0 copy-start.9
  6.6 0.0 copy-start.5
  6.6 0.0 all-gather.2.cloned.1.call-start
  6.6 0.7 all-gather.2.cloned.1.call-update
  7.3 1.8 stack.2
  9.2 14.3 %all-to-all-start = ((bf16[32,2,288,16]{2,3,1,0:T(8,128)(2,1)}), bf16[32,2,288,16]{2,3,1,0:T(8,128)(2,1)}, u32[]{:S(2)}, u32[]{:S(2)}) async-start(bf16[32,2,288,16]{2,3,1,0:T(8,128)(2,1)} %stack.2), calls=%async_computation | async-start | bytes 1572864 | tf_op jit(solution)/shard_map/all_to_all | solution.py:55
  23.4 0.0 all-reduce.2.cloned.1.call-start
  23.5 0.0 copy-done.8
  23.5 0.6 reduce-window.19
  24.1 0.2 slice_reduce_fusion
  24.3 0.0 copy-done.12
  24.3 0.0 copy-done.13
  24.4 0.2 reduce-window.18
  24.5 0.0 copy-done.6
  24.6 0.0 copy-start.7
  24.6 0.0 copy-done.1
  24.6 0.7 gather_fusion
  25.3 0.1 convert_reduce_fusion
  25.3 0.0 copy-done.9
  25.4 0.1 select_reduce_fusion.2
  25.4 0.0 copy-done.5
  25.5 3.6 fusion.42
  29.0 14.5 %all-to-all-done = bf16[32,2,288,16]{2,3,1,0:T(8,128)(2,1)} async-done(((bf16[32,2,288,16]{2,3,1,0:T(8,128)(2,1)}), bf16[32,2,288,16]{2,3,1,0:T(8,128)(2,1)}, u32[]{:S(2)}, u32[]{:S(2)}) %all-to-all-start) | async-done | bytes 589856 | tf_op jit(solution)/shard_map/all_to_all | solution.py:55
  43.5 1.7 gather_fusion.1
  45.3 0.0 copy-done.7
  45.3 89.3 %all-gather.2.cloned.1.call-done = bf16[64,16,2304]{2,1,0:T(8,128)(2,1)} async-done(((bf16[2,16,2304]{2,1,0:T(8,128)(2,1)}), bf16[64,16,2304]{2,1,0:T(8,128)(2,1)}) %all-gather.2.cloned.1.call-update) | async-done | bytes 4718608 | tf_op jit(solution)/shard_map/all_gather | solution.py:58
  134.6 4.0 gather_fusion.2
  138.6 0.6 broadcast_in_dim.27
  139.2 0.0 slice-start
  139.2 3.9 fusion.1
  143.2 0.0 all-reduce.2.cloned.1.call-update
  143.2 0.1 copy.34
  143.3 0.0 slice-done
  143.3 0.1 add_bitcast_fusion
  143.4 69.9 %all-reduce.2.cloned.1.call-done = bf16[256,2304]{1,0:T(8,128)(2,1)} async-done(((bf16[256,2304]{1,0:T(8,128)(2,1)}), bf16[256,2304]{1,0:T(8,128)(2,1)}) %all-reduce.2.cloned.1.call-update) | async-done | bytes 1179664 | tf_op jit(solution)/shard_map/psum | solution.py:78
  213.4 3.6 convert_add_fusion
  216.9 0.0 copy-done.2
  216.9 0.0 copy-done.3
  216.9 1.2 convolution_convert_fusion.1
  218.1 1.6 copy.35
  219.7 0.0 copy-start.10
  219.7 91.9 %all_to_all.15 = bf16[32,20,2304]{2,1,0:T(8,128)(2,1)S(1)} all-to-all(bf16[32,20,2304]{2,1,0:T(8,128)(2,1)S(1)} %copy.35), channel_id=1, replica_groups=mesh['req'=32,'tp'=8] {'req'}, dimensions={0} | all-to-all | bytes 5898240 | tf_op jit(solution)/shard_map/all_to_all | solution.py:106
  311.6 1.8 copy-done.4
  313.5 0.0 copy-done.10
  313.5 3.8 fusion.6
  317.2 0.0 copy-done
  317.2 11.1 %convolution_convert_fusion = bf16[32,20,2304]{2,0,1:T(8,128)(2,1)} fusion(bf16[1,720,2304]{2,1,0:T(8,128)(2,1)S(1)} %copy-done, f32[32,20,720]{2,0,1:T(8,128)} %fusion.6, bf16[1,2304,720]{1,2,0:T(8,128)(2,1)} %param.28, bf16[32,20,2304]{2,1,0:T(8,128)(2,1)} %copy-done.4), kind=kOutput, calls=%fused_computation.3 | convolution fusion | flops 4250972160 | bytes 14376960 | tf_op jit(solution)/shard_map/nqf,fd->nqd/dot_general | solution.py:110
  328.3 5.3 %copy.38 = bf16[32,20,2304]{2,1,0:T(8,128)(2,1)} copy(bf16[32,20,2304]{2,0,1:T(8,128)(2,1)} %convolution_convert_fusion) | data formatting | bytes 5898240 | tf_op jit(solution)/shard_map/convert_element_type | solution.py:119
  333.6 8.3 %all-to-all-start.2 = ((bf16[32,20,2304]{2,1,0:T(8,128)(2,1)}), bf16[32,20,2304]{2,1,0:T(8,128)(2,1)}, u32[]{:S(2)}, u32[]{:S(2)}) async-start(bf16[32,20,2304]{2,1,0:T(8,128)(2,1)} %copy.38), calls=%async_computation.2 | async-start | bytes 7077888 | tf_op jit(solution)/shard_map/all_to_all | solution.py:118
  341.9 0.3 reduce-scatter.4.cloned.1.call-start
  342.2 0.0 copy-done.11
  342.2 2.2 select_reduce_fusion.1
  344.5 65.8 %all-to-all-done.2 = bf16[32,20,2304]{2,1,0:T(8,128)(2,1)} async-done(((bf16[32,20,2304]{2,1,0:T(8,128)(2,1)}), bf16[32,20,2304]{2,1,0:T(8,128)(2,1)}, u32[]{:S(2)}, u32[]{:S(2)}) %all-to-all-start.2) | async-done | bytes 2949152 | tf_op jit(solution)/shard_map/all_to_all | solution.py:118
  410.3 6.8 %fusion.2 = bf16[2304,256]{1,0:T(8,128)(2,1)} fusion(bf16[32,20,2304]{2,1,0:T(8,128)(2,1)} %all-to-all-done.2, f32[32,256]{1,0:T(8,128)S(1)} %broadcast_bitcast_fusion, s32[32,20]{0,1:T(8,128)S(1)} %copy.34, s32[32,256]{1,0:T(8,128)S(1)} %broadcast_bitcast_fusion.1, pred[32,256]{1,0:T(8,128)(4,1)S(1)} %broadcast_bitcast_fusion.2), kind=kOutput, calls=%fused_computation.9 | convolution fusion | flops 4530929664 | bytes 4205056 | tf_op jit(solution)/shard_map/hqt,hqd->td/dot_general | solution.py:121
  417.1 0.0 reduce-scatter.4.cloned.1.call-update
  417.1 44.9 %reduce-scatter.4.cloned.1.call-done = bf16[288,256]{1,0:T(8,128)(2,1)} async-done(((bf16[2304,256]{1,0:T(8,128)(2,1)}), bf16[288,256]{1,0:T(8,128)(2,1)}) %reduce-scatter.4.cloned.1.call-update) | async-done | bytes 147472
  462.0 1.1 copy.43
  463.0 1.9 add_convert_fusion
  464.9 1.7 copy.41
  (23 shorter events, 0.1 us)
Async XLA Ops:
  6.5 310.7 %copy-start = (bf16[1,720,2304]{2,1,0:T(8,128)(2,1)S(1)}, bf16[1,720,2304]{2,1,0:T(8,128)(2,1)}, u32[]{:S(2)}) copy-start(bf16[1,720,2304]{2,1,0:T(8,128)(2,1)} %param.29) | copy-start | bytes 9953284
  6.5 16.9 %copy-start.8 = (s32[256,2]{0,1:T(2,128)S(1)}, s32[256,2]{0,1:T(2,128)}, u32[]{:S(2)}) copy-start(s32[256,2]{0,1:T(2,128)} %param.26) | copy-start | bytes 6148
  6.5 17.8 %copy-start.12 = (s32[16]{0:T(128)S(1)}, s32[16]{0:T(128)}, u32[]{:S(2)}) copy-start(s32[16]{0:T(128)} %param.21) | copy-start | bytes 196
  6.5 17.8 %copy-start.13 = (s32[1,4]{1,0:T(1,128)S(1)}, s32[1,4]{1,0:T(1,128)}, u32[]{:S(2)}) copy-start(s32[1,4]{1,0:T(1,128)} %param.22) | copy-start | bytes 52
  6.5 18.0 %copy-start.6 = (bf16[2304]{0:T(1024)(128)(2,1)S(1)}, bf16[2304]{0:T(1024)(128)(2,1)}, u32[]{:S(2)}) copy-start(bf16[2304]{0:T(1024)(128)(2,1)} %param.24) | copy-start | bytes 13828
  6.5 18.0 %copy-start.1 = (s32[64]{0:T(128)S(1)}, s32[64]{0:T(128)}, u32[]{:S(2)}) copy-start(s32[64]{0:T(128)} %param.20) | copy-start | bytes 772
  6.6 18.8 %copy-start.9 = (s32[1,4]{1,0:T(1,128)S(1)}, s32[1,4]{1,0:T(1,128)}, u32[]{:S(2)}) copy-start(s32[1,4]{1,0:T(1,128)} %param.23) | copy-start | bytes 52
  6.6 18.9 %copy-start.5 = (bf16[256,288]{0,1:T(8,128)(2,1)S(1)}, bf16[256,288]{0,1:T(8,128)(2,1)}, u32[]{:S(2)}) copy-start(bf16[256,288]{0,1:T(8,128)(2,1)} %param.16) | copy-start | bytes 442372
  6.6 128.0 %all-gather.2.cloned.1.call-start = ((), (), s32[]{:S(2)}) async-start(), calls=%async_computation.4 | async-start | bytes 4866048 | tf_op jit(solution)/shard_map/all_gather | solution.py:58
  9.2 34.4 %all-to-all-start = ((bf16[32,2,288,16]{2,3,1,0:T(8,128)(2,1)}), bf16[32,2,288,16]{2,3,1,0:T(8,128)(2,1)}, u32[]{:S(2)}, u32[]{:S(2)}) async-start(bf16[32,2,288,16]{2,3,1,0:T(8,128)(2,1)} %stack.2), calls=%async_computation | async-start | bytes 1572864 | tf_op jit(solution)/shard_map/all_to_all | solution.py:55
  23.4 189.9 %all-reduce.2.cloned.1.call-start = ((), (), s32[]{:S(2)}) async-start(), calls=%async_computation.5 | async-start | bytes 2359296 | tf_op jit(solution)/shard_map/psum | solution.py:78
  24.6 20.7 %copy-start.7 = (s32[8,3]{0,1:T(4,128)}, s32[8,3]{0,1:T(4,128)S(1)}, u32[]{:S(2)}) copy-start(s32[8,3]{0,1:T(4,128)S(1)} %reduce-window.20) | copy-start | bytes 292
  139.2 4.1 slice-start
  213.3 3.6 copy-start.2
  213.3 3.6 copy-start.3
  219.7 93.7 %copy-start.10 = (bf16[1,2304,720]{1,2,0:T(8,128)(2,1)S(1)}, bf16[1,2304,720]{1,2,0:T(8,128)(2,1)}, u32[]{:S(2)}) copy-start(bf16[1,2304,720]{1,2,0:T(8,128)(2,1)} %param.27) | copy-start | bytes 9953284
  311.6 1.8 copy-start.4
  333.6 8.6 %copy-start.11 = (bf16[2304,8]{0,1:T(8,128)(2,1)S(1)}, bf16[2304,8]{0,1:T(8,128)(2,1)}, u32[]{:S(2)}) copy-start(bf16[2304,8]{0,1:T(8,128)(2,1)} %param.25) | copy-start | bytes 110596
  333.6 76.6 %all-to-all-start.2 = ((bf16[32,20,2304]{2,1,0:T(8,128)(2,1)}), bf16[32,20,2304]{2,1,0:T(8,128)(2,1)}, u32[]{:S(2)}, u32[]{:S(2)}) async-start(bf16[32,20,2304]{2,1,0:T(8,128)(2,1)} %copy.38), calls=%async_computation.2 | async-start | bytes 7077888 | tf_op jit(solution)/shard_map/all_to_all | solution.py:118
  341.9 120.0 %reduce-scatter.4.cloned.1.call-start = ((), (), s32[]{:S(2)}) async-start(), calls=%async_computation.6 | async-start | bytes 1327104
Sparse Core Ops, SparseCore 0:
  10.9 123.6 all-gather.1
  143.3 69.9 all-reduce.1
  417.2 44.7 reduce-scatter.3
